TPU v7x, 256 devices: a whole 4x4x8 slice. The times are simulated.
256 devices in a mesh: gx: 4 (over z_hi), gy: 8 (over z_lo, x), gz: 8 (over y, core).
Axes of the slice: x: 4, y: 4, z: 8 (z_hi: 4, z_lo: 2; z = z_hi * 2 + z_lo), core: 2. Of those that a mesh axis runs over, the one named last changes fastest.
Arguments:
- positions: float32 [3, 8, 8, 16, 8], P(None, 'gx', 'gy', 'gz'), as said below
- features: float32 [8, 8, 16, 8, 128], P('gx', 'gy', 'gz'), may hold values from -6 to 6
- species: int32 [8, 8, 16, 8], P('gx', 'gy', 'gz'), may hold values from 0 to 4
- centers: int32 [8192], P(('gx', 'gy', 'gz')), may hold values from 0 to 32, as said below
- neighbours: int32 [8192, 32], P(('gx', 'gy', 'gz')), may hold values from 0 to 384, as said below
- counts: int32 [256], P(('gx', 'gy', 'gz')), may hold values from 0 to 32, as said below
- species_scale: float32 [5], replicated, may hold values from 0.5 to 2
- species_shift: float32 [5], replicated, may hold values from -4 to 4
- center_weight: float32 [128, 128], replicated, may hold values from -0.5 to 0.5
- near_weight: float32 [128, 128], replicated, may hold values from -0.5 to 0.5
- basis_weight: float32 [8, 128], replicated, may hold values from -12 to 12
- path_weight: float32 [3, 128], replicated, may hold values from -6 to 6
- value_weight: float32 [128, 256], replicated, may hold values from -0.5 to 0.5
- latent_weight: float32 [256, 128], replicated, may hold values from -0.375 to 0.375
- out_weight: float32 [128], replicated, may hold values from -0.5 to 0.5
Outputs:
- site_energy: float32 [8, 8, 16, 8], P('gx', 'gy', 'gz')
- forces: float32 [3, 8, 8, 16, 8], P(None, 'gx', 'gy', 'gz')
- virial: float32 [9, 8, 8, 16, 8], P(None, 'gx', 'gy', 'gz')
Inputs may be any that keep to these rules, and one draw needn't show every extreme that they name: `positions`: a listed neighbour lies within two lattice steps of its center, closer than 4.95 Angstrom; coordinates are the site's place in the cell plus a small jitter. `centers`: domain d's block of 32 entries lists its occupied own slots in increasing order, then 32 in the rest. `neighbours`: row k of domain d's block holds the frame rows of the occupied sites within two lattice steps of center k, in any order, and 384 in the other entries; rows of padding centers are all 384. counts[d] is the number of entries of domain d's block of centers that are not 32; some domain holds 32.
All inputs are finite; a program needn't handle non-finite values.
Results may differ from a plain program's by a relative error of at most 0.0003.
Values sent between devices are 32-bit elements; how exact they have to be, the bound alone decides.
A program may use at most 64 MiB of HBM per device.

v0:
```python
import math

import jax
import jax.numpy as jnp
from jax import lax
from jax.sharding import PartitionSpec as P

EXACT_DOT = lax.Precision.HIGHEST
CUTOFF = 5.0
CELL_SIDE = 4.6
ROOT_HALF = 0.7071067811865476


def padded(array, sides, width):
    for axis, dim in sides:
        size, length = (lax.axis_size(axis), array.shape[dim])
        up = [(i, (i + 1) % size) for i in range(size)]
        down = [(j, i) for i, j in up]
        last = lax.slice_in_dim(array, length - width, length, axis=dim)
        leading = lax.slice_in_dim(array, 0, width, axis=dim)
        before = lax.ppermute(last, axis, up)
        after = lax.ppermute(leading, axis, down)
        array = jnp.concatenate([before, array, after], axis=dim)
    return array


def envelope(ratio):
    polynomial = 1.0 - 28.0 * ratio**6 + 48.0 * ratio**7 - 21.0 * ratio**8
    return jnp.where(ratio < 1.0, polynomial, 0.0)


def harmonics(unit):
    along_x = unit[..., 0]
    along_y = unit[..., 1]
    along_z = unit[..., 2]
    root_three = math.sqrt(3.0)
    root_fifteen = math.sqrt(15.0)
    root_five = math.sqrt(5.0)
    return jnp.stack(
        [
            jnp.ones_like(along_x),
            root_three * along_x,
            root_three * along_y,
            root_three * along_z,
            root_fifteen * along_x * along_y,
            root_fifteen * along_y * along_z,
            0.5 * root_five * (3.0 * along_z * along_z - 1.0),
            root_fifteen * along_x * along_z,
            0.5 * root_fifteen * (along_x * along_x - along_y * along_y),
        ],
        axis=-1,
    )


def path_table(path_weight):
    width = path_weight.shape[1]
    return jnp.concatenate(
        [
            path_weight[0:1],
            jnp.broadcast_to(path_weight[1:2], (3, width)),
            jnp.broadcast_to(path_weight[2:3], (5, width)),
        ],
        axis=0,
    )


def center_energy(
    displace,
    live,
    center_proj,
    near_proj,
    scale,
    shift,
    active,
    basis_weight,
    paths,
    value_weight,
    latent_weight,
    out_weight,
):
    width = center_proj.shape[-1]
    neighbours_count = displace.shape[1]
    length = jnp.sqrt(jnp.sum(displace * displace, axis=-1))
    ratio = length / CUTOFF
    weight = envelope(ratio) * live
    frequency = jnp.arange(1, basis_weight.shape[0] + 1).astype(jnp.float32) * math.pi
    basis = math.sqrt(2.0 / CUTOFF) * jnp.sin(ratio[..., None] * frequency) / length[..., None]
    angular = harmonics(displace / length[..., None])
    radial = jnp.einsum("knb,bc->knc", basis, basis_weight, precision=EXACT_DOT)
    latent = weight[..., None] * jax.nn.silu(radial + center_proj[:, None, :] + near_proj)
    mixed = jnp.einsum("knc,cd->knd", latent, value_weight, precision=EXACT_DOT)
    values = mixed[..., :width]
    env_weight = mixed[..., width:]
    embed = jnp.einsum("knc,knm->kcm", env_weight, angular, precision=EXACT_DOT) / math.sqrt(
        neighbours_count
    )
    weighted = embed * jnp.transpose(paths)[None]
    inner = jnp.einsum("knm,kcm->knc", angular, weighted, precision=EXACT_DOT)
    scalars = values * inner
    joined = jnp.concatenate([latent, scalars], axis=-1)
    update = jax.nn.silu(jnp.einsum("knc,cd->knd", joined, latent_weight, precision=EXACT_DOT))
    final = (latent + weight[..., None] * update) * ROOT_HALF
    pair_energy = jnp.einsum("knc,c->kn", final, out_weight, precision=EXACT_DOT)
    return active * (scale * jnp.sum(pair_energy, axis=1) / math.sqrt(neighbours_count) + shift)


def own_to_frame(slots, cells_x, cells_y, cells_z, sites):
    owned = cells_x * cells_y * cells_z * sites
    frame_count = (cells_x + 2) * (cells_y + 2) * (cells_z + 2) * sites
    site = slots % sites
    cell = slots // sites
    cell_z = cell % cells_z
    cell_y = cell // cells_z % cells_y
    cell_x = cell // (cells_z * cells_y)
    frame = (
        ((cell_x + 1) * (cells_y + 2) + cell_y + 1) * (cells_z + 2) + cell_z + 1
    ) * sites + site
    return jnp.where(slots < owned, frame, frame_count)


def cell_corner(span_x, span_y, span_z):
    grid_x = jnp.broadcast_to(
        jnp.arange(span_x).astype(jnp.float32)[:, None, None], (span_x, span_y, span_z)
    )
    grid_y = jnp.broadcast_to(
        jnp.arange(span_y).astype(jnp.float32)[None, :, None], (span_x, span_y, span_z)
    )
    grid_z = jnp.broadcast_to(
        jnp.arange(span_z).astype(jnp.float32)[None, None, :], (span_x, span_y, span_z)
    )
    return (jnp.stack([grid_x, grid_y, grid_z], axis=-1) * CELL_SIDE)[:, :, :, None, :]


def pair_return(totals, centre_rows, near_rows, displace, pair_grad):
    block = displace.shape[0]
    slots_count = displace.shape[1]
    pair_virial = -(displace[..., :, None] * pair_grad[..., None, :]).reshape(block, slots_count, 9)
    centre_part = jnp.concatenate(
        [jnp.sum(pair_grad, axis=1), 0.5 * jnp.sum(pair_virial, axis=1)], axis=-1
    )
    near_part = jnp.concatenate([-pair_grad, 0.5 * pair_virial], axis=-1).reshape(
        block * slots_count, 12
    )
    totals = totals.at[centre_rows].add(centre_part)
    return totals.at[near_rows.reshape(-1)].add(near_part)


def local(
    positions,
    features,
    species,
    centers,
    neighbours,
    counts,
    species_scale,
    species_shift,
    center_weight,
    near_weight,
    basis_weight,
    path_weight,
    value_weight,
    latent_weight,
    out_weight,
):
    cells_x, cells_y, cells_z, sites, width = features.shape
    owned = cells_x * cells_y * cells_z * sites
    span_x = cells_x + 2
    span_y = cells_y + 2
    span_z = cells_z + 2
    frame_count = span_x * span_y * span_z * sites
    coords = jnp.transpose(positions, (1, 2, 3, 4, 0)).reshape(
        cells_x, cells_y, cells_z, 1, sites * 3
    )
    coords = jnp.pad(coords, ((0, 0), (0, 0), (0, 0), (0, 0), (0, width - sites * 3)))
    payload = jnp.concatenate([features, coords], axis=3)
    framed = padded(payload, (("gx", 0), ("gy", 1), ("gz", 2)), 1)
    frame_feat = framed[:, :, :, :sites, :].reshape(frame_count, width)
    in_cell = framed[:, :, :, sites, : sites * 3].reshape(span_x, span_y, span_z, sites, 3)
    frame_position = (in_cell + cell_corner(span_x, span_y, span_z)).reshape(frame_count, 3)
    frame_position = jnp.concatenate([frame_position, jnp.zeros((1, 3), jnp.float32)], axis=0)
    near = jnp.dot(frame_feat, near_weight, precision=EXACT_DOT, preferred_element_type=jnp.float32)
    near = jnp.concatenate([near, jnp.zeros((1, width), jnp.float32)], axis=0)
    own_center = jnp.dot(
        features.reshape(owned, width),
        center_weight,
        precision=EXACT_DOT,
        preferred_element_type=jnp.float32,
    )
    own_center = jnp.concatenate([own_center, jnp.zeros((1, width), jnp.float32)], axis=0)
    own_species = jnp.concatenate([species.reshape(owned), jnp.zeros((1,), jnp.int32)], axis=0)
    kinds = jnp.arange(species_scale.shape[0])
    paths = path_table(path_weight)
    dead_shift = jnp.array([6.0, 0.0, 0.0], jnp.float32)
    block = min(32, owned)

    def visit(step_index, carry):
        totals, energy = carry
        start = (jnp.asarray(step_index) * block).astype(jnp.int32)
        active = (start + jnp.arange(block) < counts[0]).astype(jnp.float32)
        kind = own_species[centers]
        matches = (kind[:, None] == kinds[None, :]).astype(jnp.float32)
        scale = jnp.sum(matches * species_scale[None, :], axis=1)
        shift = jnp.sum(matches * species_shift[None, :], axis=1)
        centre_rows = own_to_frame(centers, cells_x, cells_y, cells_z, sites)
        live = (neighbours != frame_count).astype(jnp.float32)
        separation = frame_position[neighbours] - frame_position[centre_rows][:, None, :]
        displace = jnp.where(live[..., None] > 0.0, separation, dead_shift)
        center_proj = own_center[centers]
        near_proj = near[neighbours]

        def energy_of(moved):
            return center_energy(
                moved,
                live,
                center_proj,
                near_proj,
                scale,
                shift,
                active,
                basis_weight,
                paths,
                value_weight,
                latent_weight,
                out_weight,
            )

        energies, pull = jax.vjp(energy_of, displace)
        pair_grad = pull(jnp.ones_like(energies))[0]
        totals = pair_return(totals, centre_rows, neighbours, displace, pair_grad)
        energy = energy.at[centers].add(energies)
        return (totals, energy)

    initial = (jnp.zeros((frame_count + 1, 12), jnp.float32), jnp.zeros((owned + 1,), jnp.float32))
    limit = owned // block
    totals, energy = lax.fori_loop(0, limit, visit, initial)
    grid = totals[:frame_count].reshape(span_x, span_y, span_z, sites * 12)
    outgoing = jnp.stack([grid[:, :, 0], grid[:, :, span_z - 1]], axis=2)
    incoming = padded(outgoing, (("gz", 2),), 1)
    grid = grid[:, :, 1 : span_z - 1]
    grid = grid.at[:, :, 0].add(incoming[:, :, 0])
    grid = grid.at[:, :, cells_z - 1].add(incoming[:, :, 3])
    outgoing = jnp.stack([grid[:, 0], grid[:, span_y - 1]], axis=1)
    incoming = padded(outgoing, (("gy", 1),), 1)
    grid = grid[:, 1 : span_y - 1]
    grid = grid.at[:, 0].add(incoming[:, 0])
    grid = grid.at[:, cells_y - 1].add(incoming[:, 3])
    outgoing = jnp.stack([grid[0], grid[span_x - 1]], axis=0)
    incoming = padded(outgoing, (("gx", 0),), 1)
    grid = grid[1 : span_x - 1]
    grid = grid.at[0].add(incoming[0])
    grid = grid.at[cells_x - 1].add(incoming[3])
    grid = grid.reshape(cells_x, cells_y, cells_z, sites, 12)
    forces = jnp.transpose(grid[..., 0:3], (4, 0, 1, 2, 3))
    virial = jnp.transpose(grid[..., 3:12], (4, 0, 1, 2, 3))
    site_energy = energy[:owned].reshape(cells_x, cells_y, cells_z, sites)
    return (site_energy, forces, virial)


def solution(mesh):
    placed = (
        P(None, "gx", "gy", "gz", None),
        P("gx", "gy", "gz", None, None),
        P("gx", "gy", "gz", None),
        P(("gx", "gy", "gz")),
        P(("gx", "gy", "gz"), None),
        P(("gx", "gy", "gz")),
        P(),
        P(),
        P(),
        P(),
        P(),
        P(),
        P(),
        P(),
        P(),
    )
    return jax.shard_map(
        local,
        mesh=mesh,
        in_specs=placed,
        out_specs=(
            P("gx", "gy", "gz", None),
            P(None, "gx", "gy", "gz", None),
            P(None, "gx", "gy", "gz", None),
        ),
        check_vma=False,
    )
```

profile of v0, /device:TPU:70, one launch (start us, length us, event | category | flops | bytes accessed | tf_op | source)
XLA Modules:
  0.0 83.8 jit_solution(17809172024784964686)
XLA Ops:
  2.2 4.6 %collective-permute-start = (f32[1,1,2,9,128]{4,3,2,1,0:T(8,128)S(1)}, f32[1,1,2,9,128]{4,3,2,1,0:T(8,128)S(1)}, u32[]{:S(2)}, u32[]{:S(2)}) collective-permute-start(f32[1,1,2,9,128]{4,3,2,1,0:T(8,128)S(1)} %get-tuple-element.173), channel_id=1, source_target_pairs={{0,64},{64,128},{128,192},{192,0},{1,65},{65,129},{129,193},{193,1... | collective-permute-start | bytes 27656 | tf_op jit(solution)/shard_map/ppermute | solution.py:21
  10.4 2.2 %collective-permute-done.1 = f32[1,1,2,9,128]{4,3,2,1,0:T(8,128)S(1)} collective-permute-done((f32[1,1,2,9,128]{4,3,2,1,0:T(8,128)S(1)}, f32[1,1,2,9,128]{4,3,2,1,0:T(8,128)S(1)}, u32[]{:S(2)}, u32[]{:S(2)}) %collective-permute-start.1) | collective-permute-done | bytes 9248 | tf_op jit(solution)/shard_map/ppermute | solution.py:22
  13.5 3.3 %collective-permute-start.2 = (f32[4,1,2,9,128]{4,3,2,1,0:T(8,128)S(1)}, f32[4,1,2,9,128]{4,3,2,1,0:T(8,128)S(1)}, u32[]{:S(2)}, u32[]{:S(2)}) collective-permute-start(f32[4,1,2,9,128]{4,3,2,1,0:T(8,128)S(1)} %pad_maximum_fusion.3), channel_id=1, source_target_pairs={{0,8},{8,16},{16,24},{24,32},{32,40},{40,48},{48,56},{56,0},{1,9},... | collective-permute-start | bytes 110600 | tf_op jit(solution)/shard_map/ppermute | solution.py:21
  16.8 2.2 %collective-permute-done.3 = f32[4,1,2,9,128]{4,3,2,1,0:T(8,128)S(1)} collective-permute-done((f32[4,1,2,9,128]{4,3,2,1,0:T(8,128)S(1)}, f32[4,1,2,9,128]{4,3,2,1,0:T(8,128)S(1)}, u32[]{:S(2)}, u32[]{:S(2)}) %collective-permute-start.3) | collective-permute-done | bytes 36896 | tf_op jit(solution)/shard_map/ppermute | solution.py:22
  19.1 2.9 %collective-permute-start.5 = (f32[4,3,1,9,128]{4,3,2,1,0:T(8,128)S(1)}, f32[4,3,1,9,128]{4,3,2,1,0:T(8,128)S(1)}, u32[]{:S(2)}, u32[]{:S(2)}) collective-permute-start(f32[4,3,1,9,128]{4,3,2,1,0:T(8,128)S(1)} %get-tuple-element.168), channel_id=1, source_target_pairs={{1,0},{2,1},{3,2},{4,3},{5,4},{6,5},{7,6},{0,7},{9,8},{10,9},{11,1... | collective-permute-start | bytes 165896 | tf_op jit(solution)/shard_map/ppermute | solution.py:22
  23.3 1.1 %collective-permute-done.4 = f32[4,3,1,9,128]{4,3,2,1,0:T(8,128)S(1)} collective-permute-done((f32[4,3,1,9,128]{4,3,2,1,0:T(8,128)S(1)}, f32[4,3,1,9,128]{4,3,2,1,0:T(8,128)S(1)}, u32[]{:S(2)}, u32[]{:S(2)}) %collective-permute-start.4) | collective-permute-done | bytes 55328 | tf_op jit(solution)/shard_map/ppermute | solution.py:21
  26.5 2.8 %gather_fusion.1 = f32[1024,3]{1,0:T(8,128)S(1)} fusion(f32[385,3]{1,0:T(8,128)S(1)} %concatenate.60, s32[1024]{0:T(1024)S(1)} %broadcast_clamp_fusion), kind=kCustom, calls=%fused_computation.1 | custom fusion | bytes 28672 | tf_op jit(solution)/shard_map/while/body/eval_jaxpr/gather | solution.py:206
  30.5 3.0 %gather_fusion.4 = f32[1024,128]{1,0:T(8,128)S(1)} fusion(f32[385,128]{1,0:T(8,128)S(1)} %concatenate.62, s32[1024]{0:T(1024)S(1)} %broadcast_clamp_fusion), kind=kCustom, calls=%fused_computation.4 | custom fusion | bytes 1052672 | tf_op jit(solution)/shard_map/while/body/eval_jaxpr/gather | solution.py:209
  34.2 1.5 %broadcast_multiply_fusion = (f32[32,32,128]{2,1,0:T(8,128)S(1)}, f32[32,32,128]{2,1,0:T(8,128)S(1)}) fusion(f32[32,32]{1,0:T(8,128)S(1)} %get-tuple-element.178, f32[32,32,128]{2,1,0:T(8,128)S(1)} %bitcast.73, f32[32,128]{1,0:T(8,128)S(1)} %gather_fusion.3, f32[8,128]{1,0:T(8,128)S(1)} %copy-done.12, f32[32,32]{1,0:T(8,128)S(1)} %get-tuple-element.179, ...), kind=kOutput, calls=%fused_computation.69 | convolution fusion | flops 13524992 | bytes 1605664 | tf_op jit(solution)/shard_map/while/body/eval_jaxpr/jvp(knb,bc->knc)/dot_general | solution.py:89
  37.3 1.1 %slice_multiply_fusion.2 = (f32[32,32,128]{2,1,0:T(8,128)S(1)}, f32[32,32,128]{2,1,0:T(8,128)S(1)}) fusion(f32[32,32,256]{2,1,0:T(8,128)S(1)} %fusion.62, f32[32,128,9]{1,2,0:T(8,128)S(1)} %convolution_multiply_fusion.1, f32[32,32,9]{1,0,2:T(8,128)S(1)} %constant_dynamic-update-slice_fusion), kind=kOutput, calls=%fused_computation.53 | convolution fusion | flops 14286848 | bytes 1757184 | tf_op jit(solution)/shard_map/while/body/eval_jaxpr/jvp(knm,kcm->knc)/dot_general | solution.py:98
  38.4 1.0 %fusion.2 = f32[32,32,128]{2,1,0:T(8,128)S(1)} fusion(f32[32,32,128]{2,1,0:T(8,128)S(1)} %get-tuple-element.193, f32[32,32,128]{2,1,0:T(8,128)S(1)} %get-tuple-element.191, f32[256,128]{1,0:T(8,128)S(1)} %copy-done.3), kind=kOutput, calls=%fused_computation.14 | convolution fusion | flops 402915328 | bytes 1703936 | tf_op jit(solution)/shard_map/while/body/eval_jaxpr/jvp(knc,cd->knd)/dot_general | solution.py:101
  39.4 2.2 %fusion.26 = f32[1,32,32]{2,0,1:T(1,128)S(1)} fusion(f32[32,32,128]{2,1,0:T(8,128)S(1)} %get-tuple-element.191, f32[32,32]{1,0:T(8,128)S(1)} %get-tuple-element.178, f32[32,32,128]{2,1,0:T(8,128)S(1)} %fusion.2, f32[128]{0:T(128)S(1)} %copy-done.11), kind=kOutput, calls=%fused_computation.40 | convolution fusion | flops 2490368 | bytes 1057280 | tf_op jit(solution)/shard_map/while/body/eval_jaxpr/jvp(knc,c->kn)/dot_general | solution.py:103
  42.1 1.0 %fusion.15 = f32[32,32,256]{2,1,0:T(8,128)S(1)} fusion(f32[32,32,128]{2,1,0:T(8,128)S(1)} %fusion.2, f32[32,32]{1,0:T(8,128)S(1)} %get-tuple-element.177, f32[128]{0:T(128)S(1)} %copy-done.11, f32[32]{0:T(128)S(1)} %get-tuple-element.187, f32[256,128]{1,0:T(8,128)S(1)} %copy-done.3), kind=kOutput, calls=%fused_computation.31 | convolution fusion | flops 404094976 | bytes 1708672 | tf_op jit(solution)/shard_map/while/body/eval_jaxpr/transpose(jvp(knc,cd->knd))/dot_general | solution.py:101
  45.8 1.1 %fusion.35 = f32[32,32,128]{2,1,0:T(8,128)S(1)} fusion(f32[32,128,9]{1,2,0:T(8,128)S(1)} %fusion.1, f32[32,32,9]{1,0,2:T(8,128)S(1)} %constant_dynamic-update-slice_fusion), kind=kOutput, calls=%fused_computation.55 | convolution fusion | flops 14155776 | bytes 708608 | tf_op jit(solution)/shard_map/while/body/eval_jaxpr/transpose(jvp(knc,knm->kcm))/dot_general | solution.py:94
  46.9 1.1 %multiply_reduce_fusion = (f32[32,32]{1,0:T(8,128)S(1)}, f32[32,32,128]{2,1,0:T(8,128)S(1)}) fusion(f32[32,32,128]{2,1,0:T(8,128)S(1)} %get-tuple-element.192, f32[128,256]{1,0:T(8,128)S(1)} %copy-done, f32[32,32,128]{2,1,0:T(8,128)S(1)} %slice_multiply_fusion, f32[32,32,128]{2,1,0:T(8,128)S(1)} %fusion.35, f32[32,32,256]{2,1,0:T(8,128)S(1)} %fusion.15, ...), kind=kOutput, calls=%fused_computation.36 | convolution fusion | flops 404225024 | bytes 2757248 | tf_op jit(solution)/shard_map/while/body/eval_jaxpr/transpose(jvp(knc,cd->knd))/dot_general | solution.py:91
  48.0 2.7 %fusion.55 = (f32[32,32]{1,0:T(8,128)S(1)}, f32[32,32]{1,0:T(8,128)S(1)}) fusion(f32[32,32]{1,0:T(8,128)S(1)} %get-tuple-element.175, f32[8]{0:T(128)S(1)} %convert_multiply_fusion, f32[32,32]{1,0:T(8,128)S(1)} %get-tuple-element.176, f32[32,32]{1,0:T(8,128)S(1)} %get-tuple-element.179, f32[8,128]{1,0:T(8,128)S(1)} %copy-done.12, ...), kind=kOutput, calls=%fused_computation.83 | convolution fusion | flops 13973504 | bytes 1077280 | tf_op jit(solution)/shard_map/while/body/eval_jaxpr/transpose(jvp(knb,bc->knc))/dot_general | solution.py:89
  52.2 6.7 %scatter_fusion = f32[385,12]{1,0:T(8,128)S(1)} fusion(f32[385,12]{1,0:T(8,128)S(1)} %scatter_custom_fusion.1, s32[1024]{0:T(1024)S(1)} %bitcast.81, f32[1024,12]{1,0:T(8,128)S(1)} %bitcast.69), kind=kCustom, calls=%fused_computation.7 | custom fusion | flops 12288 | bytes 151552 | tf_op jit(solution)/shard_map/while/body/eval_jaxpr/scatter-add | solution.py:145
  59.2 2.8 %collective-permute-start.7 = (f32[4,3,1,96]{3,2,1,0:T(1,128)S(1)}, f32[4,3,1,96]{3,2,1,0:T(1,128)S(1)}, u32[]{:S(2)}, u32[]{:S(2)}) collective-permute-start(f32[4,3,1,96]{3,2,1,0:T(1,128)S(1)} %get-tuple-element.171), channel_id=1, source_target_pairs={{1,0},{2,1},{3,2},{4,3},{5,4},{6,5},{7,6},{0,7},{9,8},{10,9},{11,1... | collective-permute-start | bytes 13832 | tf_op jit(solution)/shard_map/ppermute | solution.py:22
  62.0 1.3 %collective-permute-done.6 = f32[4,3,1,96]{3,2,1,0:T(1,128)S(1)} collective-permute-done((f32[4,3,1,96]{3,2,1,0:T(1,128)S(1)}, f32[4,3,1,96]{3,2,1,0:T(1,128)S(1)}, u32[]{:S(2)}, u32[]{:S(2)}) %collective-permute-start.6) | collective-permute-done | bytes 4640 | tf_op jit(solution)/shard_map/ppermute | solution.py:21
  63.4 3.9 %collective-permute-start.8 = (f32[4,1,2,96]{3,2,1,0:T(2,128)S(1)}, f32[4,1,2,96]{3,2,1,0:T(2,128)S(1)}, u32[]{:S(2)}, u32[]{:S(2)}) collective-permute-start(f32[4,1,2,96]{3,2,1,0:T(2,128)S(1)} %get-tuple-element.180), channel_id=1, source_target_pairs={{0,8},{8,16},{16,24},{24,32},{32,40},{40,48},{48,56},{56,0},{1,9},... | collective-permute-start | bytes 9224 | tf_op jit(solution)/shard_map/ppermute | solution.py:21
  67.3 1.3 %collective-permute-done.8 = f32[4,1,2,96]{3,2,1,0:T(2,128)S(1)} collective-permute-done((f32[4,1,2,96]{3,2,1,0:T(2,128)S(1)}, f32[4,1,2,96]{3,2,1,0:T(2,128)S(1)}, u32[]{:S(2)}, u32[]{:S(2)}) %collective-permute-start.8) | collective-permute-done | bytes 3104 | tf_op jit(solution)/shard_map/ppermute | solution.py:21
  68.6 4.4 %collective-permute-done.9 = f32[4,1,2,96]{3,2,1,0:T(2,128)S(1)} collective-permute-done((f32[4,1,2,96]{3,2,1,0:T(2,128)S(1)}, f32[4,1,2,96]{3,2,1,0:T(2,128)S(1)}, u32[]{:S(2)}, u32[]{:S(2)}) %collective-permute-start.9) | collective-permute-done | bytes 3104 | tf_op jit(solution)/shard_map/ppermute | solution.py:22
  73.0 2.2 %collective-permute-start.10 = (f32[1,1,2,96]{3,2,1,0:T(2,128)S(1)}, f32[1,1,2,96]{3,2,1,0:T(2,128)S(1)}, u32[]{:S(2)}, u32[]{:S(2)}) collective-permute-start(f32[1,1,2,96]{3,2,1,0:T(2,128)S(1)} %get-tuple-element.183), channel_id=1, source_target_pairs={{0,64},{64,128},{128,192},{192,0},{1,65},{65,129},{129,193},{193,1... | collective-permute-start | bytes 2312 | tf_op jit(solution)/shard_map/ppermute | solution.py:21
  77.6 4.8 %collective-permute-done.11 = f32[1,1,2,96]{3,2,1,0:T(2,128)S(1)} collective-permute-done((f32[1,1,2,96]{3,2,1,0:T(2,128)S(1)}, f32[1,1,2,96]{3,2,1,0:T(2,128)S(1)}, u32[]{:S(2)}, u32[]{:S(2)}) %collective-permute-start.11) | collective-permute-done | bytes 800 | tf_op jit(solution)/shard_map/ppermute | solution.py:22
  (139 shorter events, 21.0 us)
Async XLA Ops:
  0.6 35.1 %copy-start = (f32[128,256]{1,0:T(8,128)S(1)}, f32[128,256]{1,0:T(8,128)}, u32[]{:S(2)}) copy-start(f32[128,256]{1,0:T(8,128)} %param.40) | copy-start | bytes 393220
  1.5 0.7 copy-start.1
  2.2 4.6 %copy-start.2 = (s32[32,32]{1,0:T(8,128)S(1)}, s32[32,32]{1,0:T(8,128)}, u32[]{:S(2)}) copy-start(s32[32,32]{1,0:T(8,128)} %param.32) | copy-start | bytes 12292
  2.2 8.2 %collective-permute-start = (f32[1,1,2,9,128]{4,3,2,1,0:T(8,128)S(1)}, f32[1,1,2,9,128]{4,3,2,1,0:T(8,128)S(1)}, u32[]{:S(2)}, u32[]{:S(2)}) collective-permute-start(f32[1,1,2,9,128]{4,3,2,1,0:T(8,128)S(1)} %get-tuple-element.173), channel_id=1, source_target_pairs={{0,64},{64,128},{128,192},{192,0},{1,65},{65,129},{129,193},{193,1... | collective-permute-start | bytes 27656 | tf_op jit(solution)/shard_map/ppermute | solution.py:21
  6.7 5.8 %collective-permute-start.1 = (f32[1,1,2,9,128]{4,3,2,1,0:T(8,128)S(1)}, f32[1,1,2,9,128]{4,3,2,1,0:T(8,128)S(1)}, u32[]{:S(2)}, u32[]{:S(2)}) collective-permute-start(f32[1,1,2,9,128]{4,3,2,1,0:T(8,128)S(1)} %get-tuple-element.174), channel_id=1, source_target_pairs={{64,0},{128,64},{192,128},{0,192},{65,1},{129,65},{193,129},{1,193... | collective-permute-start | bytes 27656 | tf_op jit(solution)/shard_map/ppermute | solution.py:22
  6.9 0.7 copy-start.6
  7.6 0.7 copy-start.7
  8.4 0.8 %copy-start.5 = (f32[128,128]{1,0:T(8,128)S(1)}, f32[128,128]{1,0:T(8,128)}, u32[]{:S(2)}) copy-start(f32[128,128]{1,0:T(8,128)} %param.36) | copy-start | bytes 196612
  9.3 0.7 copy-start.10
  12.6 6.5 %collective-permute-start.3 = (f32[4,1,2,9,128]{4,3,2,1,0:T(8,128)S(1)}, f32[4,1,2,9,128]{4,3,2,1,0:T(8,128)S(1)}, u32[]{:S(2)}, u32[]{:S(2)}) collective-permute-start(f32[4,1,2,9,128]{4,3,2,1,0:T(8,128)S(1)} %pad_maximum_fusion.3), channel_id=1, source_target_pairs={{8,0},{16,8},{24,16},{32,24},{40,32},{48,40},{56,48},{0,56},{9,1},... | collective-permute-start | bytes 110600 | tf_op jit(solution)/shard_map/ppermute | solution.py:22
  13.5 5.5 %collective-permute-start.2 = (f32[4,1,2,9,128]{4,3,2,1,0:T(8,128)S(1)}, f32[4,1,2,9,128]{4,3,2,1,0:T(8,128)S(1)}, u32[]{:S(2)}, u32[]{:S(2)}) collective-permute-start(f32[4,1,2,9,128]{4,3,2,1,0:T(8,128)S(1)} %pad_maximum_fusion.3), channel_id=1, source_target_pairs={{0,8},{8,16},{16,24},{24,32},{32,40},{40,48},{48,56},{56,0},{1,9},... | collective-permute-start | bytes 110600 | tf_op jit(solution)/shard_map/ppermute | solution.py:21
  19.1 5.3 %collective-permute-start.4 = (f32[4,3,1,9,128]{4,3,2,1,0:T(8,128)S(1)}, f32[4,3,1,9,128]{4,3,2,1,0:T(8,128)S(1)}, u32[]{:S(2)}, u32[]{:S(2)}) collective-permute-start(f32[4,3,1,9,128]{4,3,2,1,0:T(8,128)S(1)} %get-tuple-element.167), channel_id=1, source_target_pairs={{0,1},{1,2},{2,3},{3,4},{4,5},{5,6},{6,7},{7,0},{8,9},{9,10},{10,1... | collective-permute-start | bytes 165896 | tf_op jit(solution)/shard_map/ppermute | solution.py:21
  19.1 5.2 %collective-permute-start.5 = (f32[4,3,1,9,128]{4,3,2,1,0:T(8,128)S(1)}, f32[4,3,1,9,128]{4,3,2,1,0:T(8,128)S(1)}, u32[]{:S(2)}, u32[]{:S(2)}) collective-permute-start(f32[4,3,1,9,128]{4,3,2,1,0:T(8,128)S(1)} %get-tuple-element.168), channel_id=1, source_target_pairs={{1,0},{2,1},{3,2},{4,3},{5,4},{6,5},{7,6},{0,7},{9,8},{10,9},{11,1... | collective-permute-start | bytes 165896 | tf_op jit(solution)/shard_map/ppermute | solution.py:22
  24.5 0.8 %copy-start.4 = (f32[128,128]{1,0:T(8,128)S(1)}, f32[128,128]{1,0:T(8,128)}, u32[]{:S(2)}) copy-start(f32[128,128]{1,0:T(8,128)} %param.37) | copy-start | bytes 196612
  29.6 0.7 copy-start.8
  33.5 0.7 copy-start.12
  37.3 1.1 %copy-start.3 = (f32[256,128]{1,0:T(8,128)S(1)}, f32[256,128]{1,0:T(8,128)}, u32[]{:S(2)}) copy-start(f32[256,128]{1,0:T(8,128)} %param.41) | copy-start | bytes 393220
  38.4 1.0 %copy-start.11 = (f32[128]{0:T(128)S(1)}, f32[128]{0:T(128)}, u32[]{:S(2)}) copy-start(f32[128]{0:T(128)} %param.42) | copy-start | bytes 1540
  59.0 4.3 %collective-permute-start.6 = (f32[4,3,1,96]{3,2,1,0:T(1,128)S(1)}, f32[4,3,1,96]{3,2,1,0:T(1,128)S(1)}, u32[]{:S(2)}, u32[]{:S(2)}) collective-permute-start(f32[4,3,1,96]{3,2,1,0:T(1,128)S(1)} %get-tuple-element.172), channel_id=1, source_target_pairs={{0,1},{1,2},{2,3},{3,4},{4,5},{5,6},{6,7},{7,0},{8,9},{9,10},{10,1... | collective-permute-start | bytes 13832 | tf_op jit(solution)/shard_map/ppermute | solution.py:21
  59.2 4.1 %collective-permute-start.7 = (f32[4,3,1,96]{3,2,1,0:T(1,128)S(1)}, f32[4,3,1,96]{3,2,1,0:T(1,128)S(1)}, u32[]{:S(2)}, u32[]{:S(2)}) collective-permute-start(f32[4,3,1,96]{3,2,1,0:T(1,128)S(1)} %get-tuple-element.171), channel_id=1, source_target_pairs={{1,0},{2,1},{3,2},{4,3},{5,4},{6,5},{7,6},{0,7},{9,8},{10,9},{11,1... | collective-permute-start | bytes 13832 | tf_op jit(solution)/shard_map/ppermute | solution.py:22
  63.4 5.2 %collective-permute-start.8 = (f32[4,1,2,96]{3,2,1,0:T(2,128)S(1)}, f32[4,1,2,96]{3,2,1,0:T(2,128)S(1)}, u32[]{:S(2)}, u32[]{:S(2)}) collective-permute-start(f32[4,1,2,96]{3,2,1,0:T(2,128)S(1)} %get-tuple-element.180), channel_id=1, source_target_pairs={{0,8},{8,16},{16,24},{24,32},{32,40},{40,48},{48,56},{56,0},{1,9},... | collective-permute-start | bytes 9224 | tf_op jit(solution)/shard_map/ppermute | solution.py:21
  67.3 5.7 %collective-permute-start.9 = (f32[4,1,2,96]{3,2,1,0:T(2,128)S(1)}, f32[4,1,2,96]{3,2,1,0:T(2,128)S(1)}, u32[]{:S(2)}, u32[]{:S(2)}) collective-permute-start(f32[4,1,2,96]{3,2,1,0:T(2,128)S(1)} %get-tuple-element.181), channel_id=1, source_target_pairs={{8,0},{16,8},{24,16},{32,24},{40,32},{48,40},{56,48},{0,56},{9,1},... | collective-permute-start | bytes 9224 | tf_op jit(solution)/shard_map/ppermute | solution.py:22
  73.0 4.5 %collective-permute-start.10 = (f32[1,1,2,96]{3,2,1,0:T(2,128)S(1)}, f32[1,1,2,96]{3,2,1,0:T(2,128)S(1)}, u32[]{:S(2)}, u32[]{:S(2)}) collective-permute-start(f32[1,1,2,96]{3,2,1,0:T(2,128)S(1)} %get-tuple-element.183), channel_id=1, source_target_pairs={{0,64},{64,128},{128,192},{192,0},{1,65},{65,129},{129,193},{193,1... | collective-permute-start | bytes 2312 | tf_op jit(solution)/shard_map/ppermute | solution.py:21
  76.7 5.7 %collective-permute-start.11 = (f32[1,1,2,96]{3,2,1,0:T(2,128)S(1)}, f32[1,1,2,96]{3,2,1,0:T(2,128)S(1)}, u32[]{:S(2)}, u32[]{:S(2)}) collective-permute-start(f32[1,1,2,96]{3,2,1,0:T(2,128)S(1)} %get-tuple-element.182), channel_id=1, source_target_pairs={{64,0},{128,64},{192,128},{0,192},{65,1},{129,65},{193,129},{1,193... | collective-permute-start | bytes 2312 | tf_op jit(solution)/shard_map/ppermute | solution.py:22
  (2 other events, 1.3 us)
where the time goes:
time: 84.2 us; the launch traced here: 83.8 us
  starting transfers between devices  21.6 us (26%)
  waiting for transfers between devices  17.3 us (21%)
  local copies, waits for them, and re-layouts  17.1 us (20%)
  matrix products  16.1 us (19%)
  other arithmetic  9.77 us (12%)
  between operations  1.9 us (2%)
    ppermute x6, starting transfers between devices, padded(): before = lax.ppermute(last, axis, up)  14.2 us
    ppermute x6, waiting for transfers between devices, padded(): after = lax.ppermute(leading, axis, down)  13.6 us
    ppermute x6, starting transfers between devices, padded(): after = lax.ppermute(leading, axis, down)  7.43 us
    scatter-add x1, other arithmetic, pair_return(): return totals.at[near_rows.reshape(-1)].add(near_part)  6.66 us
    unnamed x30, local copies, waits for them, and re-layouts  5.41 us
    dot_general x2, matrix products, center_energy(): radial = jnp.einsum('knb,bc->knc', basis, basis_weight, precision=EXACT_DOT)  4.16 us
    ppermute x6, waiting for transfers between devices, padded(): before = lax.ppermute(last, axis, up)  3.78 us
    gather x2, local copies, waits for them, and re-layouts, visit(): frame_position[neighbours] - frame_position[centre_rows][:, None, :]  3.08 us
  transfers between devices with their start and end apart: 12, of which 8 were waited for; matrix products, arithmetic and copies ran while one was open for 4% of the time, Pallas kernels for 0%

commit v1 on v0

v1 whole, which is shorter than its diff:
```python
import functools
import math

import jax
import jax.numpy as jnp
import numpy as np
from jax import lax
from jax.experimental import pallas as pl
from jax.experimental.pallas import tpu as pltpu
from jax.sharding import PartitionSpec as P

MESH = pl.DeviceIdType.MESH
F32 = jnp.float32
BF16 = jnp.bfloat16
CUTOFF = 5.0
CELL_SIDE = 4.6
ROOT_HALF = 0.7071067811865476
CHANNELS = 128
PAIRS = 1024
DIRECTIONS = [(a, b, c) for a in (-1, 0, 1) for b in (-1, 0, 1) for c in (-1, 0, 1)]
HOME = 13


def offsets():
    steps = range(-2, 3)
    return [
        (i, j, k)
        for i in steps
        for j in steps
        for k in steps
        if 0 < i * i + j * j + k * k <= 4
    ]


@functools.cache
def tables():
    rows = np.zeros(PAIRS, np.int32)
    column = np.zeros(2 * PAIRS, np.int32)
    site = np.zeros(2 * PAIRS, np.int32)
    domain = np.zeros(PAIRS, np.int32)
    slot = np.zeros(PAIRS, np.int32)
    shift = np.zeros((8, PAIRS), np.float32)
    for own in range(32):
        cell, inner = divmod(own, 8)
        at = (2 + 2 * (cell // 2) + inner // 4, 2 + inner // 2 % 2, 2 + 2 * (cell % 2) + inner % 2)
        for number, step in enumerate(offsets()):
            pair = own * 32 + number
            x, y, z = (u + v for u, v in zip(at, step))
            near_site = x % 2 * 4 + y % 2 * 2 + z % 2
            cx, cy, cz = x // 2, y // 2, z // 2
            rows[pair] = ((cx * 3 + cy) * 4 + cz) * 8 + near_site
            toward_x = -1 if cx == 0 else int(cx == 3)
            toward_z = -1 if cz == 0 else int(cz == 3)
            domain[pair] = (toward_x + 1) * 9 + cy * 3 + toward_z + 1
            near_cell = (cx - 1 - 2 * toward_x) * 2 + (cz - 1 - 2 * toward_z)
            slot[pair] = near_cell * 8 + near_site
            column[pair] = domain[pair] * 8 + near_cell
            column[PAIRS + pair] = HOME * 8 + cell
            site[pair] = near_site
            site[PAIRS + pair] = inner
            for axis in range(3):
                shift[axis, pair] = CELL_SIDE * ((x, y, z)[axis] // 2 - at[axis] // 2)
    pair = np.arange(PAIRS)
    own = pair // 32
    lane = np.arange(128)
    gather = rows[:, None] == np.arange(384)[None]
    from_domain = (domain[None] == np.arange(32)[:, None])
    pick = np.concatenate(
        [
            lane[:, None] % 32 == slot[None],
            lane[:, None] % 32 == own[None],
        ],
        axis=0,
    )
    scatter = np.arange(216)[:, None] == column[None]
    sites = np.arange(8)[:, None] == site[None]
    spread = np.zeros((128, 384), np.float32)
    for m in range(9):
        spread[8 + m, m:128:16] = 1.0
        spread[40 + m, 128 + m : 256 : 16] = 1.0
    spread[17, 256:] = 1.0
    spread[49, 256:] = 1.0
    return dict(
        gather=gather.astype(jnp.bfloat16),
        scatter=scatter.astype(jnp.bfloat16),
        pick=pick.astype(jnp.bfloat16),
        from_domain=from_domain.astype(np.float32),
        sites=sites.astype(np.float32),
        shift=shift,
        listed=rows.reshape(32, 32).astype(np.int32),
        spread=spread.astype(jnp.bfloat16),
    )


def mul(a, b):
    return lax.dot_general(a, b, (((1,), (0,)), ((), ())), preferred_element_type=F32)


def mul_t(a, b):
    return lax.dot_general(a, b, (((1,), (1,)), ((), ())), preferred_element_type=F32)


def split(a):
    high = a.astype(BF16)
    return high, (a - high.astype(F32)).astype(BF16)


def split3(a):
    high = a.astype(BF16)
    rest = a - high.astype(F32)
    mid = rest.astype(BF16)
    return high, mid, (rest - mid.astype(F32)).astype(BF16)


def iota(shape, axis):
    return lax.broadcasted_iota(jnp.int32, shape, axis)


def halves(a):
    return a[:, :CHANNELS] + a[:, CHANNELS:]


def beside(*parts):
    return jnp.concatenate(parts, axis=1)


def above(*parts):
    return jnp.concatenate(parts, axis=0)


def project(rows, weight_high, weight_low):
    high, low = split(rows)
    stacked = above(
        beside(weight_high, weight_low), beside(weight_high, jnp.zeros_like(weight_low))
    )
    return halves(mul(beside(high, low), stacked))


def position_row(positions):
    repeat = (iota((8, 128), 0) == iota((8, 128), 1) % 8).astype(F32).astype(BF16)
    spread = sum(mul(part, repeat) for part in split3(positions))
    own = iota((12, 128), 1) // 8 == iota((12, 128), 0)
    return jnp.sum(jnp.where(own, spread, 0.0), axis=0, keepdims=True)


def by_component(rows):
    lanes = iota(rows.shape, 1) // 32
    return above(*[jnp.where(lanes == axis, rows, 0.0) for axis in range(3)])


def listed_pairs(centers, counts, neighbours, listed):
    place = iota((32, 32), 1)
    names = jnp.where(place < counts, centers, 32) == iota((32, 32), 0)
    names = names.astype(F32)
    occupied = jnp.sum(names, axis=1, keepdims=True)
    name_bits = names.astype(BF16)
    entries = neighbours.astype(F32)
    coarse = jnp.floor(entries * (1.0 / 32.0))
    fine = entries - 32.0 * coarse
    by_slot = 32.0 * mul(name_bits, coarse.astype(BF16)) + mul(name_bits, fine.astype(BF16))
    wanted = listed.astype(F32)
    found = jnp.zeros((32, 32), F32)
    for entry in range(32):
        found = jnp.where(by_slot[:, entry : entry + 1] == wanted, 1.0, found)
    found = found * occupied
    spread_out = (iota((32, PAIRS), 1) % 32 == iota((32, PAIRS), 0)).astype(F32).astype(BF16)
    wide = mul(found.astype(BF16), spread_out)
    own = iota((32, PAIRS), 1) // 32 == iota((32, PAIRS), 0)
    return jnp.sum(jnp.where(own, wide, 0.0), axis=0, keepdims=True), occupied


def geometry(displace, live):
    dx = jnp.where(live > 0.0, displace[0:1], 6.0)
    dy = jnp.where(live > 0.0, displace[1:2], 0.0)
    dz = jnp.where(live > 0.0, displace[2:3], 0.0)
    length = jnp.sqrt(dx * dx + dy * dy + dz * dz)
    inverse = 1.0 / length
    ratio = length * (1.0 / CUTOFF)
    square = ratio * ratio
    fourth = square * square
    inside = ratio < 1.0
    weight = 1.0 + fourth * square * (-28.0 + ratio * (48.0 - 21.0 * ratio))
    weight = jnp.where(inside, weight, 0.0) * live
    gap = 1.0 - ratio
    slope = jnp.where(inside, (-168.0 / CUTOFF) * fourth * ratio * gap * gap, 0.0) * live
    frequency = (iota((8, PAIRS), 0) + 1).astype(F32) * math.pi
    phase = frequency * ratio
    scale = math.sqrt(2.0 / CUTOFF)
    basis = scale * jnp.sin(phase) * inverse
    basis_slope = (scale / CUTOFF * frequency * jnp.cos(phase) - basis) * inverse
    ex, ey, ez = dx * inverse, dy * inverse, dz * inverse
    three, fifteen, five = math.sqrt(3.0), math.sqrt(15.0), math.sqrt(5.0)
    angular = above(
        jnp.ones_like(ex),
        three * ex,
        three * ey,
        three * ez,
        fifteen * ex * ey,
        fifteen * ey * ez,
        0.5 * five * (3.0 * ez * ez - 1.0),
        fifteen * ex * ez,
        0.5 * fifteen * (ex * ex - ey * ey),
    )
    return dict(
        d=(dx, dy, dz), e=(ex, ey, ez), inverse=inverse, weight=weight, slope=slope,
        basis=basis, basis_slope=basis_slope, angular=angular,
    )


def pair_gradient(geo, grad_basis, grad_weight, grad_angular):
    ex, ey, ez = geo["e"]
    three, fifteen, five = math.sqrt(3.0), math.sqrt(15.0), math.sqrt(5.0)
    g = [grad_angular[m : m + 1] for m in range(9)]
    radial = grad_weight * geo["slope"] + jnp.sum(
        grad_basis * geo["basis_slope"], axis=0, keepdims=True
    )
    ux = three * g[1] + fifteen * (g[4] * ey + g[7] * ez + g[8] * ex)
    uy = three * g[2] + fifteen * (g[4] * ex + g[5] * ez - g[8] * ey)
    uz = three * g[3] + fifteen * (g[5] * ey + g[7] * ex) + 3.0 * five * g[6] * ez
    along = radial - geo["inverse"] * (ux * ex + uy * ey + uz * ez)
    return tuple(along * e + geo["inverse"] * u for e, u in zip((ex, ey, ez), (ux, uy, uz)))


def parcels(d, grad, sites, scatter):
    virial = [-0.5 * a * b for a in d for b in grad]
    near = [-g for g in grad] + virial
    home = list(grad) + virial
    near_sites, home_sites = sites[:, :PAIRS], sites[:, PAIRS:]
    zero = jnp.zeros((32, 2 * PAIRS), F32)
    stacked = above(
        beside(
            above(*[near_sites * part for part in near]),
            above(*[home_sites * part for part in home]),
        ),
        zero,
    )
    high, low = split(stacked)
    return mul_t(scatter, high) + mul_t(scatter, low)


def interactions(
    geo, near_rows, own_proj, pull_rows, gather, spread, basis_weight, paths, weights, own_rows
):
    (value_high, value_low, latent_high, latent_low, latent_t_high, latent_t_low,
     value_t_high, value_t_low) = weights
    stack = above(geo["basis"], geo["angular"], geo["weight"], jnp.zeros((14, PAIRS), F32))
    high = stack.astype(BF16).astype(F32)
    stack = above(high, stack - high, jnp.zeros((64, PAIRS), F32))
    scalars = jnp.transpose(stack).astype(BF16)
    basis_high, basis_low = split(basis_weight)
    near_high, near_low = split(near_rows)
    blank = jnp.zeros((24, CHANNELS), BF16)
    basis_rows = above(
        beside(basis_high, basis_low),
        beside(blank, blank),
        beside(basis_high, jnp.zeros_like(basis_low)),
        beside(blank, blank),
        jnp.zeros((64, 256), BF16),
    )
    table = above(beside(near_high, near_low), basis_rows)
    same_center = iota((256, 128), 0) // 32 == iota((256, 128), 1) // 16
    same_center_t = iota((128, 256), 1) // 32 == iota((128, 256), 0) // 16
    readout = above(
        beside(basis_weight, jnp.zeros((8, CHANNELS), F32)),
        beside(jnp.zeros((8, CHANNELS), F32), jnp.ones((8, CHANNELS), F32)),
    )
    readout_high, readout_low = split(readout)
    angular = above(geo["angular"], jnp.zeros((7, PAIRS), F32))
    sums, grad_scalars, grad_angulars = [], [], []
    for block in range(4):
        at = slice(block * 256, block * 256 + 256)
        rows = scalars[at]
        wide = mul(rows, spread)
        y_t_high = jnp.where(same_center, wide[:, :128], 0.0).astype(BF16)
        y_t_low = jnp.where(same_center, wide[:, 128:256], 0.0).astype(BF16)
        y_t = beside(y_t_high, y_t_low)
        y = jnp.where(same_center_t, above(*[angular[:, at]] * 8), 0.0)
        y_high, y_low = split(y)
        u = wide[:, 256:]
        h = halves(mul(beside(gather[at], rows), table)) + own_rows(own_proj, block)
        gate = jax.nn.sigmoid(h)
        silu = h * gate
        latent = u * silu
        l_high, l_low = split(latent)
        mixed = mul(beside(l_high, l_low), above(value_high, value_high)) + mul(l_high, value_low)
        value, env = mixed[:, :128], mixed[:, 128:]
        env_high, env_low = split(env)
        gamma = halves(mul(y_high, beside(env_high, env_low))) + mul(y_low, env_high)
        path = paths * gamma
        path_high, path_low = split(path)
        stacked = above(beside(path_high, path_low), beside(path_high, jnp.zeros_like(path_low)))
        inner = halves(mul(y_t, stacked))
        scalar = value * inner
        s_high, s_low = split(scalar)
        q = halves(mul(beside(l_high, s_high), beside(latent_high, latent_low)))
        q = q + mul(beside(l_low, s_low), latent_high)
        q_gate = jax.nn.sigmoid(q)
        update = q * q_gate
        sums.append(jnp.sum((latent + u * update).reshape(8, 32, CHANNELS), axis=1))
        pull = own_rows(pull_rows, block)
        grad_q = u * pull * (q_gate * (1.0 + q - update))
        g_high, g_low = split(grad_q)
        grad_joined = mul(beside(g_high, g_low), above(latent_t_high, latent_t_high))
        grad_joined = grad_joined + mul(g_high, latent_t_low)
        grad_latent = pull + grad_joined[:, :128]
        grad_scalar = grad_joined[:, 128:]
        grad_value = grad_scalar * inner
        grad_inner = grad_scalar * value
        i_high, i_low = split(grad_inner)
        grad_path = halves(mul(y_high, beside(i_high, i_low))) + mul(y_low, i_high)
        grad_gamma = paths * grad_path
        c_high, c_low = split(grad_gamma)
        stacked = above(beside(c_high, c_low), beside(c_high, jnp.zeros_like(c_low)))
        grad_env = halves(mul(y_t, stacked))
        v_high, v_low = split(grad_value)
        e_high, e_low = split(grad_env)
        grad_latent = grad_latent + halves(
            mul(beside(v_high, e_high), beside(value_t_high, value_t_low))
        ) + mul(beside(v_low, e_low), value_t_high)
        grad_h = grad_latent * u * (gate * (1.0 + h - silu))
        grad_u = pull * update + grad_latent * silu
        h_high, h_low = split(grad_h)
        u_high, u_low = split(grad_u)
        both = beside(h_high, u_high)
        grad_scalars.append(
            mul_t(readout_high, both)
            + mul_t(readout_high, beside(h_low, u_low))
            + mul_t(readout_low, both)
        )
        left_high, left_low = beside(path_high, c_high), beside(path_low, c_low)
        both = beside(i_high, env_high)
        cross = mul_t(left_high, both) + mul_t(left_high, beside(i_low, env_low))
        cross = cross + mul_t(left_low, both)
        cross = jnp.where(same_center_t, cross, 0.0)
        total = cross[0:16]
        for t in range(1, 8):
            total = total + cross[16 * t : 16 * t + 16]
        grad_angulars.append(total)
    return sums, beside(*grad_scalars), beside(*grad_angulars)


def path_rows(path_weight, scale):
    row = iota((128, CHANNELS), 0) % 16
    first, second, third = (path_weight[i : i + 1] for i in range(3))
    rows = jnp.where(row == 0, first, jnp.where(row < 4, second, third))
    return jnp.where(row < 9, rows, 0.0) * scale


def pull_of(occupied, species, scale, out_weight):
    return occupied * scale * out_weight * (ROOT_HALF / math.sqrt(32.0))


def of_kind(species, table):
    result = jnp.zeros(species.shape, F32)
    for kind in range(5):
        result = jnp.where(species == kind, table(kind), result)
    return result


def column_of(cells):
    rows = above(*[jnp.broadcast_to(cells[i : i + 1], (8, 8)) for i in range(4)])
    own = iota((32, 8), 0) % 8 == iota((32, 8), 1)
    return jnp.sum(jnp.where(own, rows, 0), axis=1, keepdims=True)


def row_of(column):
    eye = iota((8, 8), 0) == iota((8, 8), 1)
    return jnp.sum(jnp.where(eye, column, 0.0), axis=0, keepdims=True)


def kernel(
    shape,
    positions_ref, species_ref, centers_ref, neighbours_ref, counts_ref, scale_ref, shift_ref,
    listed_ref, cell_shift_ref,
    features_hbm, center_hbm, near_hbm, basis_hbm, path_hbm, value_hbm, latent_hbm, out_hbm,
    gather_hbm, scatter_hbm, pick_hbm, domain_hbm, sites_hbm, spread_hbm,
    energy_ref, forces_ref, virial_ref,
    frame, places, sent_place, returns, outgoing,
    center_w, near_w, basis_w, path_w, value_w, latent_w, out_w,
    gather_v, scatter_v, pick_v, domain_v, sites_v, spread_v, proj_v, pull_v,
    local_sem, send_sem, recv_sem,
):
    me = tuple(lax.axis_index(axis) for axis in ("gx", "gy", "gz"))

    def device(direction):
        return tuple(
            lax.rem(i + step + size, size) for i, step, size in zip(me, direction, shape)
        )

    others = [(i, d) for i, d in enumerate(DIRECTIONS) if i != HOME]
    barrier = pltpu.get_barrier_semaphore()
    for _, direction in others:
        pl.semaphore_signal(barrier, inc=1, device_id=device(direction), device_id_type=MESH)

    own_frame = frame.at[pl.ds(1, 2), pl.ds(1, 1), pl.ds(1, 2)]
    fetches = [(features_hbm, own_frame)] + list(
        zip(
            (center_hbm, near_hbm, basis_hbm, path_hbm, value_hbm, latent_hbm, out_hbm,
             gather_hbm, scatter_hbm, pick_hbm, domain_hbm, sites_hbm, spread_hbm),
            (center_w, near_w, basis_w, path_w, value_w, latent_w, out_w,
             gather_v, scatter_v, pick_v, domain_v, sites_v, spread_v),
        )
    )
    fetches = [
        pltpu.make_async_copy(src, dst, local_sem.at[i]) for i, (src, dst) in enumerate(fetches)
    ]
    for copy in fetches:
        copy.start()

    sent_place[...] = jnp.broadcast_to(
        position_row(positions_ref[...].reshape(12, 8)), (8, 128)
    )
    pl.semaphore_wait(barrier, 26)

    def span(step):
        return {1: (slice(1, 2), slice(0, 1)), -1: (slice(0, 1), slice(3, 4)), 0: (slice(0, 2), slice(1, 3))}[step]

    sends = []
    for index, (a, b, c) in others:
        (from_x, to_x), (from_z, to_z) = span(a), span(c)
        to_y = 1 - b
        sends.append(
            pltpu.make_async_remote_copy(
                src_ref=features_hbm.at[from_x, slice(0, 1), from_z],
                dst_ref=frame.at[to_x, slice(to_y, to_y + 1), to_z],
                send_sem=send_sem.at[index],
                recv_sem=recv_sem.at[index],
                device_id=device((a, b, c)),
                device_id_type=MESH,
            )
        )
        sends.append(
            pltpu.make_async_remote_copy(
                src_ref=sent_place,
                dst_ref=places.at[26 - index],
                send_sem=send_sem.at[27 + index],
                recv_sem=recv_sem.at[27 + index],
                device_id=device((a, b, c)),
                device_id_type=MESH,
            )
        )
    for copy in sends:
        copy.start()

    live, occupied = listed_pairs(
        centers_ref[...], counts_ref[...], neighbours_ref[...], listed_ref[...]
    )
    for copy in fetches:
        copy.wait()
    species = column_of(species_ref[...].reshape(4, 8))
    scale = of_kind(species, lambda kind: scale_ref[kind])
    shift = of_kind(species, lambda kind: shift_ref[kind])
    pull_v[...] = occupied * scale * out_w[...] * (ROOT_HALF / math.sqrt(32.0))
    own = frame[1:3, 1:2, 1:3].reshape(32, CHANNELS)
    proj_v[...] = project(own, *split(center_w[...]))
    own_place = sum(
        mul(part, pick_v[128:256]) for part in split3(by_component(sent_place[0:1]))
    )
    base = cell_shift_ref[0:3] - own_place
    value, latent = value_w[...], latent_w[...]
    weights = (
        split(value) + split(latent) + split(jnp.transpose(latent)) + split(jnp.transpose(value))
    )
    near_high, near_low = split(near_w[...])
    paths = path_rows(path_w[...], 1.0 / math.sqrt(32.0))

    for copy in sends:
        copy.wait_recv()

    near_rows = project(frame[...].reshape(384, CHANNELS), near_high, near_low)
    place_rows = above(
        jnp.concatenate([places[i, 0:1] for i in range(HOME)], axis=0),
        sent_place[0:1],
        jnp.concatenate([places[i, 0:1] for i in range(HOME + 1, 27)], axis=0),
        jnp.zeros((5, 128), F32),
    )
    gathered = sum(mul(part, pick_v[0:128]) for part in split3(by_component(place_rows)))
    chosen = above(
        *[
            jnp.sum(gathered[32 * i : 32 * i + 32] * domain_v[...], axis=0, keepdims=True)
            for i in range(3)
        ]
    )
    geo = geometry(chosen + base, live)

    def own_rows(ref, block):
        return above(
            *[
                jnp.broadcast_to(ref[pl.ds(block * 8 + t, 1), :], (32, CHANNELS))
                for t in range(8)
            ]
        )

    sums, grad_scalars, grad_angular = interactions(
        geo, near_rows, proj_v, pull_v, gather_v[...], spread_v[...], basis_w[...], paths,
        weights, own_rows,
    )
    grad = pair_gradient(geo, grad_scalars[0:8], grad_scalars[8:9], grad_angular)
    outgoing[...] = halves_of(parcels(geo["d"], grad, sites_v[...], scatter_v[...]))

    backs = []
    for index, direction in others:
        backs.append(
            pltpu.make_async_remote_copy(
                src_ref=outgoing.at[index],
                dst_ref=returns.at[26 - index],
                send_sem=send_sem.at[54 + index],
                recv_sem=recv_sem.at[54 + index],
                device_id=device(direction),
                device_id_type=MESH,
            )
        )
    for copy in backs:
        copy.start()

    for block in range(4):
        at = slice(block * 8, block * 8 + 8)
        energy = jnp.sum(sums[block] * out_w[...], axis=1, keepdims=True)
        energy = energy * (ROOT_HALF / math.sqrt(32.0))
        energy = occupied[at] * (scale[at] * energy + shift[at])
        energy_ref[block // 2, 0, block % 2 : block % 2 + 1, :] = row_of(energy)

    for copy in sends:
        copy.wait_send()
    for copy in backs:
        copy.wait_recv()
    total = outgoing[HOME]
    for index, _ in others:
        total = total + returns[index]
    for component in range(12):
        ref, where = (forces_ref, component) if component < 3 else (virial_ref, component - 3)
        piece = total[0:4, component * 8 : component * 8 + 8]
        for cx in range(2):
            ref[where, cx, 0] = piece[2 * cx : 2 * cx + 2]
    for copy in backs:
        copy.wait_send()


def halves_of(rows):
    return rows.reshape(27, 8, CHANNELS)


def local(shape, *arguments):
    (positions, features, species, centers, neighbours, counts, species_scale, species_shift,
     center_weight, near_weight, basis_weight, path_weight, value_weight, latent_weight,
     out_weight) = arguments
    fixed = {name: jnp.asarray(value) for name, value in tables().items()}
    vmem = pl.BlockSpec(memory_space=pltpu.VMEM)
    smem = pl.BlockSpec(memory_space=pltpu.SMEM)
    any_ = pl.BlockSpec(memory_space=pl.ANY)
    hbm = pl.BlockSpec(memory_space=pltpu.HBM)
    return pl.pallas_call(
        functools.partial(kernel, shape),
        out_shape=(
            jax.ShapeDtypeStruct((2, 1, 2, 8), F32),
            jax.ShapeDtypeStruct((3, 2, 1, 2, 8), F32),
            jax.ShapeDtypeStruct((9, 2, 1, 2, 8), F32),
        ),
        in_specs=[vmem] * 5 + [smem] * 2 + [vmem] * 2 + [any_] * 14,
        out_specs=(vmem,) * 3,
        scratch_shapes=[
            pltpu.VMEM((4, 3, 4, 8, CHANNELS), F32),
            pltpu.VMEM((27, 8, 128), F32),
            pltpu.VMEM((8, 128), F32),
            pltpu.VMEM((27, 8, 128), F32),
            pltpu.VMEM((27, 8, 128), F32),
            pltpu.VMEM((128, 128), F32),
            pltpu.VMEM((128, 128), F32),
            pltpu.VMEM((8, 128), F32),
            pltpu.VMEM((3, 128), F32),
            pltpu.VMEM((128, 256), F32),
            pltpu.VMEM((256, 128), F32),
            pltpu.VMEM((1, 128), F32),
            pltpu.VMEM((1024, 384), BF16),
            pltpu.VMEM((216, 2048), BF16),
            pltpu.VMEM((256, 1024), BF16),
            pltpu.VMEM((32, 1024), F32),
            pltpu.VMEM((8, 2048), F32),
            pltpu.VMEM((128, 384), BF16),
            pltpu.VMEM((32, 128), F32),
            pltpu.VMEM((32, 128), F32),
            pltpu.SemaphoreType.DMA((14,)),
            pltpu.SemaphoreType.DMA((81,)),
            pltpu.SemaphoreType.DMA((81,)),
        ],
        compiler_params=pltpu.CompilerParams(
            collective_id=0, has_side_effects=True, vmem_limit_bytes=56 * 1024 * 1024
        ),
        name="allegro",
    )(
        positions, species, centers.reshape(1, 32), neighbours, counts.reshape(1, 1),
        species_scale, species_shift, fixed["listed"], fixed["shift"],
        features, center_weight, near_weight, basis_weight, path_weight, value_weight,
        latent_weight, out_weight.reshape(1, 128), fixed["gather"], fixed["scatter"],
        fixed["pick"], fixed["from_domain"], fixed["sites"], fixed["spread"],
    )


def solution(mesh):
    placed = (
        P(None, "gx", "gy", "gz", None),
        P("gx", "gy", "gz", None, None),
        P("gx", "gy", "gz", None),
        P(("gx", "gy", "gz")),
        P(("gx", "gy", "gz"), None),
        P(("gx", "gy", "gz")),
    ) + (P(),) * 9
    shape = tuple(mesh.shape[axis] for axis in ("gx", "gy", "gz"))
    return jax.shard_map(
        functools.partial(local, shape),
        mesh=mesh,
        in_specs=placed,
        out_specs=(
            P("gx", "gy", "gz", None),
            P(None, "gx", "gy", "gz", None),
            P(None, "gx", "gy", "gz", None),
        ),
        check_vma=False,
    )
```

time: 84.2 us -> 41.2 us (0.49)
  the two profiles are of different devices: /device:TPU:70 before, /device:TPU:64 now
where the time goes in v1:
time: 41.2 us; the launch traced here: 41 us
  Pallas kernels  37.1 us (90%)
  local copies, waits for them, and re-layouts  2.6 us (6%)
  between operations  1.31 us (3%)
    pallas_call x1, Pallas kernels, local(): pl.pallas_call(functools.partial(kernel, shape), out_shape=(jax.ShapeDtyp...  37.1 us
    pallas_call x1, local copies, waits for them, and re-layouts, local(): pl.pallas_call(functools.partial(kernel, shape), out_shape=(jax.ShapeDtyp...  1.42 us
    unnamed x6, local copies, waits for them, and re-layouts  1.18 us

profile of v1, /device:TPU:64, one launch (start us, length us, event | category | flops | bytes accessed | tf_op | source)
XLA Modules:
  0.0 41.0 jit_solution(10201876943158795002)
XLA Ops:
  1.3 37.1 %allegro.1 = (f32[2,1,2,8]{3,2,1,0:T(2,128)}, f32[3,2,1,2,8]{4,3,2,1,0:T(2,128)}, f32[9,2,1,2,8]{4,3,2,1,0:T(2,128)}) custom-call(f32[3,2,1,2,8]{4,3,2,1,0:T(2,128)} %positions_ref.1, s32[2,1,2,8]{3,2,1,0:T(2,128)} %species_ref.1, s32[1,32]{1,0:T(1,128)} %bitcast.4, s32[32,32]{1,0:T(8,128)} %neighbours_ref.1, s32[1,1]{1,0:T(1,128)} %bitcast.3.counts_ref, ...), custom_call_target="tpu_custom_call" | custom-call | tf_op jit(solution)/shard_map/allegro/pallas_call | solution.py:552
  38.4 0.0 copy-start.1
  38.4 0.0 copy-start
  38.4 1.4 %copy.26 = f32[9,2,1,2,8]{0,4,3,2,1:T(8,128)} copy(f32[9,2,1,2,8]{4,3,2,1,0:T(2,128)} %get-tuple-element.5) | data formatting | bytes 2304 | tf_op jit(solution)/shard_map/allegro/pallas_call | solution.py:552
  39.8 0.0 copy-done.1
  39.9 0.6 %copy.30 = f32[2,1,2,8]{3,2,1,0:T(2,128)} copy(f32[2,1,2,8]{3,2,1,0:T(2,128)S(1)} %copy-done.1) | data formatting | bytes 256
  40.4 0.0 copy-done
  40.4 0.6 %copy.31 = f32[3,2,1,2,8]{4,3,2,1,0:T(2,128)} copy(f32[3,2,1,2,8]{4,3,2,1,0:T(2,128)S(1)} %copy-done) | data formatting | bytes 768
Async XLA Ops:
  38.4 1.4 %copy-start.1 = (f32[2,1,2,8]{3,2,1,0:T(2,128)S(1)}, f32[2,1,2,8]{3,2,1,0:T(2,128)}, u32[]{:S(2)}) copy-start(f32[2,1,2,8]{3,2,1,0:T(2,128)} %get-tuple-element.9) | copy-start | bytes 388
  38.4 2.0 %copy-start = (f32[3,2,1,2,8]{4,3,2,1,0:T(2,128)S(1)}, f32[3,2,1,2,8]{4,3,2,1,0:T(2,128)}, u32[]{:S(2)}) copy-start(f32[3,2,1,2,8]{4,3,2,1,0:T(2,128)} %get-tuple-element.10) | copy-start | bytes 1156

commit v2 on v1

v2 whole, which is shorter than its diff:
```python
import functools
import math

import jax
import jax.numpy as jnp
import numpy as np
from jax import lax
from jax.experimental import pallas as pl
from jax.experimental.pallas import tpu as pltpu
from jax.sharding import PartitionSpec as P

MESH = pl.DeviceIdType.MESH
F32 = jnp.float32
BF16 = jnp.bfloat16
CUTOFF = 5.0
CELL_SIDE = 4.6
ROOT_HALF = 0.7071067811865476
CHANNELS = 128
PAIRS = 1024
DIRECTIONS = [(a, b, c) for a in (-1, 0, 1) for b in (-1, 0, 1) for c in (-1, 0, 1)]
HOME = 13
CHUNK = 1024


def offsets():
    steps = range(-2, 3)
    return [
        (i, j, k)
        for i in steps
        for j in steps
        for k in steps
        if 0 < i * i + j * j + k * k <= 4
    ]


@functools.cache
def pairs():
    result = []
    for own in range(32):
        cell, inner = divmod(own, 8)
        at = (2 + 2 * (cell // 2) + inner // 4, 2 + inner // 2 % 2, 2 + 2 * (cell % 2) + inner % 2)
        for step in offsets():
            place = tuple(u + v for u, v in zip(at, step))
            site = place[0] % 2 * 4 + place[1] % 2 * 2 + place[2] % 2
            cx, cy, cz = (u // 2 for u in place)
            row = ((cx * 3 + cy) * 4 + cz) * 8 + site
            toward_x = -1 if cx == 0 else int(cx == 3)
            toward_z = -1 if cz == 0 else int(cz == 3)
            direction = (toward_x + 1) * 9 + cy * 3 + toward_z + 1
            near_cell = (cx - 1 - 2 * toward_x) * 2 + (cz - 1 - 2 * toward_z)
            shift = [CELL_SIDE * (u // 2 - v // 2) for u, v in zip(place, at)]
            result.append((own, row, direction, near_cell * 8 + site, shift))
    return result


@functools.cache
def wanted():
    slots = [sorted({p[3] for p in pairs() if p[2] == i}) for i in range(27)]
    slots[HOME] = list(range(32))
    order = [HOME] + sorted(
        (i for i in range(27) if i != HOME),
        key=lambda i: (sum(map(bool, DIRECTIONS[i])), i),
    )
    starts, row = {}, 0
    for i in order:
        starts[i] = row
        row += len(slots[i])
    return slots, starts, order


@functools.cache
def tables():
    slots, starts, _ = wanted()
    near = np.array([starts[p[2]] + slots[p[2]].index(p[3]) for p in pairs()])
    own = np.array([p[0] for p in pairs()])
    direction = np.array([p[2] for p in pairs()])
    slot = np.array([p[3] for p in pairs()])
    lane = np.arange(128)
    shift = np.zeros((8, PAIRS), np.float32)
    shift[:3] = np.array([p[4] for p in pairs()]).T
    column = np.concatenate([direction * 4 + slot // 8, HOME * 4 + own // 8])
    site = np.concatenate([slot % 8, own % 8])
    return dict(
        gather=(near[:, None] == np.arange(256)[None]).astype(jnp.bfloat16),
        scatter=(np.arange(112)[:, None] == column[None]).astype(jnp.bfloat16),
        pick=np.concatenate(
            [lane[:, None] % 32 == slot[None], lane[:, None] % 32 == own[None]], axis=0
        ).astype(jnp.bfloat16),
        from_domain=(direction[None] == np.arange(32)[:, None]).astype(np.float32),
        sites=(np.arange(8)[:, None] == site[None]).astype(np.float32),
        shift=shift,
        listed=np.array([p[1] for p in pairs()]).reshape(32, 32).astype(np.int32),
    )


def mul(a, b):
    return lax.dot_general(a, b, (((1,), (0,)), ((), ())), preferred_element_type=F32)


def mul_t(a, b):
    return lax.dot_general(a, b, (((1,), (1,)), ((), ())), preferred_element_type=F32)


def split(a):
    high = a.astype(BF16)
    return high, (a - high.astype(F32)).astype(BF16)


def split3(a):
    high = a.astype(BF16)
    rest = a - high.astype(F32)
    mid = rest.astype(BF16)
    return high, mid, (rest - mid.astype(F32)).astype(BF16)


def iota(shape, axis):
    return lax.broadcasted_iota(jnp.int32, shape, axis)


def halves(a):
    return a[:, :CHANNELS] + a[:, CHANNELS:]


def beside(*parts):
    return jnp.concatenate(parts, axis=1)


def above(*parts):
    return jnp.concatenate(parts, axis=0)


def stack_of(high, low):
    return above(beside(high, low), beside(high, jnp.zeros_like(low)))


def project(rows, weight):
    return halves(mul(beside(*split(rows)), stack_of(*split(weight))))


def position_row(positions):
    repeat = (iota((8, 128), 0) == iota((8, 128), 1) % 8).astype(F32).astype(BF16)
    spread = sum(mul(part, repeat) for part in split3(positions))
    own = iota((12, 128), 1) // 8 == iota((12, 128), 0)
    return jnp.sum(jnp.where(own, spread, 0.0), axis=0, keepdims=True)


def by_component(rows):
    lanes = iota(rows.shape, 1) // 32
    return above(*[jnp.where(lanes == axis, rows, 0.0) for axis in range(3)])


def listed_pairs(centers, neighbours, listed):
    names = (centers == iota((32, 32), 0)).astype(F32)
    occupied = jnp.sum(names, axis=1, keepdims=True)
    name_bits = names.astype(BF16)
    entries = neighbours.astype(F32)
    coarse = jnp.floor(entries * (1.0 / 32.0))
    fine = entries - 32.0 * coarse
    by_slot = 32.0 * mul(name_bits, coarse.astype(BF16)) + mul(name_bits, fine.astype(BF16))
    wanted = listed.astype(F32)
    found = jnp.zeros((32, 32), F32)
    for entry in range(32):
        found = jnp.where(by_slot[:, entry : entry + 1] == wanted, 1.0, found)
    found = found * occupied
    spread_out = (iota((32, PAIRS), 1) % 32 == iota((32, PAIRS), 0)).astype(F32).astype(BF16)
    wide = mul(found.astype(BF16), spread_out)
    own = iota((32, PAIRS), 1) // 32 == iota((32, PAIRS), 0)
    return jnp.sum(jnp.where(own, wide, 0.0), axis=0, keepdims=True), occupied


def sine_cosine(ratio):
    angle = (ratio - 0.5) * math.pi
    square = angle * angle
    sine, cosine = jnp.zeros_like(ratio), jnp.zeros_like(ratio)
    for k in range(6, -1, -1):
        sign = (-1.0) ** k
        cosine = cosine * square + sign / math.factorial(2 * k)
        if k < 6:
            sine = sine * square + sign / math.factorial(2 * k + 1)
    return cosine, -sine * angle


def multiples(sine, cosine):
    s, c = {1: sine}, {1: cosine}
    for m in range(2, 9):
        if m % 2 == 0:
            h = m // 2
            s[m] = 2.0 * s[h] * c[h]
            c[m] = 1.0 - 2.0 * s[h] * s[h]
        else:
            a, b = m // 2, m - m // 2
            s[m] = s[a] * c[b] + c[a] * s[b]
            c[m] = c[a] * c[b] - s[a] * s[b]
    order = range(1, 9)
    return above(*[s[m] for m in order]), above(*[c[m] for m in order])


def geometry(displace, live):
    dx = jnp.where(live > 0.0, displace[0:1], 6.0)
    dy = jnp.where(live > 0.0, displace[1:2], 0.0)
    dz = jnp.where(live > 0.0, displace[2:3], 0.0)
    length = jnp.sqrt(dx * dx + dy * dy + dz * dz)
    inverse = 1.0 / length
    ratio = length * (1.0 / CUTOFF)
    square = ratio * ratio
    fourth = square * square
    inside = ratio < 1.0
    weight = 1.0 + fourth * square * (-28.0 + ratio * (48.0 - 21.0 * ratio))
    weight = jnp.where(inside, weight, 0.0) * live
    gap = 1.0 - ratio
    slope = jnp.where(inside, (-168.0 / CUTOFF) * fourth * ratio * gap * gap, 0.0) * live
    frequency = (iota((8, PAIRS), 0) + 1).astype(F32) * math.pi
    sines, cosines = multiples(*sine_cosine(jnp.minimum(ratio, 1.0)))
    scale = math.sqrt(2.0 / CUTOFF)
    basis = scale * sines * inverse
    basis_slope = (scale / CUTOFF * frequency * cosines - basis) * inverse
    ex, ey, ez = dx * inverse, dy * inverse, dz * inverse
    three, fifteen, five = math.sqrt(3.0), math.sqrt(15.0), math.sqrt(5.0)
    angular = above(
        three * ex,
        three * ey,
        three * ez,
        fifteen * ex * ey,
        fifteen * ey * ez,
        0.5 * five * (3.0 * ez * ez - 1.0),
        fifteen * ex * ez,
        0.5 * fifteen * (ex * ex - ey * ey),
    )
    return dict(
        d=(dx, dy, dz), e=(ex, ey, ez), inverse=inverse, weight=weight, slope=slope,
        basis=basis, basis_slope=basis_slope, angular=angular,
    )


def pair_gradient(geo, grad_basis, grad_weight, grad_angular):
    ex, ey, ez = geo["e"]
    three, fifteen, five = math.sqrt(3.0), math.sqrt(15.0), math.sqrt(5.0)
    g = [None] + [grad_angular[m : m + 1] for m in range(8)]
    radial = grad_weight * geo["slope"] + jnp.sum(
        grad_basis * geo["basis_slope"], axis=0, keepdims=True
    )
    ux = three * g[1] + fifteen * (g[4] * ey + g[7] * ez + g[8] * ex)
    uy = three * g[2] + fifteen * (g[4] * ex + g[5] * ez - g[8] * ey)
    uz = three * g[3] + fifteen * (g[5] * ey + g[7] * ex) + 3.0 * five * g[6] * ez
    along = radial - geo["inverse"] * (ux * ex + uy * ey + uz * ez)
    return tuple(along * e + geo["inverse"] * u for e, u in zip((ex, ey, ez), (ux, uy, uz)))


def parcels(d, grad, sites, scatter):
    virial = [-0.5 * a * b for a in d for b in grad]
    near = [-g for g in grad] + virial
    home = list(grad) + virial
    near_sites, home_sites = sites[:, :PAIRS], sites[:, PAIRS:]
    stacked = beside(
        above(*[near_sites * part for part in near]),
        above(*[home_sites * part for part in home]),
    )
    high, low = split(stacked)
    zero = jnp.zeros((32, 2 * PAIRS), BF16)
    return halves(mul_t(scatter, above(high, zero, low, zero)))


def interactions(geo, near_rows, own_proj, pull_rows, gather, basis_weight, paths, weights, chunk):
    (value_high, value_low, latent_high, latent_low, latent_t_high, latent_t_low,
     value_t_high, value_t_low) = weights
    basis_high, basis_low = split(basis_weight)
    near_high, near_low = split(near_rows)
    table = above(
        beside(near_high, near_low),
        beside(basis_high, basis_low),
        beside(basis_high, jnp.zeros_like(basis_low)),
        jnp.zeros((32, 256), BF16),
    )
    readout = above(
        beside(basis_weight, jnp.zeros((8, CHANNELS), F32)),
        beside(jnp.zeros((8, CHANNELS), F32), jnp.ones((8, CHANNELS), F32)),
    )
    readout_high, readout_low = split(readout)
    value_both = above(value_high, value_high)
    latent_both = beside(latent_high, latent_low)
    latent_t_both = above(latent_t_high, latent_t_high)
    value_t_both = beside(value_t_high, value_t_low)
    of_center = [
        (iota((8, 256), 1) // 32 == t).astype(F32) for t in range(8)
    ]
    ones = (iota((8, 256), 1) // 32 == iota((8, 256), 0)).astype(F32)
    basis_top = geo["basis"].astype(BF16).astype(F32)
    basis_rest = geo["basis"] - basis_top
    lane = iota((256, 128), 1)
    sums, grad_scalars, grad_angulars = [], [], []
    per = chunk // 256
    spare = jnp.zeros((56, 256), BF16)

    def stacked_paths(high, low):
        return above(
            beside(high, low), spare, beside(high, jnp.zeros_like(low)), spare
        )

    for first in range(0, 4, per):
        blocks = range(first, first + per)
        ys, y_ts, us, lefts = [], [], [], []
        for block in blocks:
            at = slice(block * 256, block * 256 + 256)
            angular = geo["angular"][:, at]
            y = above(*[angular * of_center[t] for t in range(8)], ones)
            flat = jnp.transpose(
                above(
                    y,
                    jnp.zeros((8, 256), F32),
                    basis_top[:, at],
                    basis_rest[:, at],
                    jnp.broadcast_to(geo["weight"][:, at], (8, 256)),
                    jnp.zeros((24, 256), F32),
                )
            )
            ys.append(split(y))
            y_ts.append(beside(*split(jnp.where(lane < 72, flat, 0.0))))
            us.append(jnp.broadcast_to(flat[:, 96:97], (256, 128)))
            radial = jnp.where((lane >= 80) & (lane < 96), flat, 0.0).astype(BF16)
            lefts.append(beside(gather[at, :128], gather[at, 128:] + radial))
        u = above(*us)
        h = halves(mul(above(*lefts), table)) + own_rows(own_proj, blocks)
        gate = jax.nn.sigmoid(h)
        silu = h * gate
        latent = u * silu
        l_high, l_low = split(latent)
        mixed = mul(beside(l_high, l_low), value_both) + mul(l_high, value_low)
        value, env = mixed[:, :128], mixed[:, 128:]
        env_high, env_low = split(env)
        inners, path_parts = [], []
        for k, block in enumerate(blocks):
            at = slice(k * 256, k * 256 + 256)
            y_high, y_low = ys[k]
            gamma = halves(mul(y_high, beside(env_high[at], env_low[at])))
            gamma = gamma + mul(y_low, env_high[at])
            parts = split(paths * gamma)
            path_parts.append(parts)
            inners.append(halves(mul(y_ts[k], stacked_paths(*parts))))
        inner = above(*inners)
        s_high, s_low = split(value * inner)
        q = halves(mul(beside(l_high, s_high), latent_both))
        q = q + mul(beside(l_low, s_low), latent_high)
        q_gate = jax.nn.sigmoid(q)
        update = q * q_gate
        sums.append(jnp.sum((latent + u * update).reshape(8 * per, 32, CHANNELS), axis=1))
        pull = own_rows(pull_rows, blocks)
        grad_q = u * pull * (q_gate * (1.0 + q - update))
        g_high, g_low = split(grad_q)
        grad_joined = mul(beside(g_high, g_low), latent_t_both) + mul(g_high, latent_t_low)
        grad_scalar = grad_joined[:, 128:]
        i_high, i_low = split(grad_scalar * value)
        v_high, v_low = split(grad_scalar * inner)
        grad_envs = []
        for k, block in enumerate(blocks):
            at = slice(k * 256, k * 256 + 256)
            y_high, y_low = ys[k]
            grad_path = halves(mul(y_high, beside(i_high[at], i_low[at])))
            grad_path = grad_path + mul(y_low, i_high[at])
            c_high, c_low = split(paths * grad_path)
            grad_envs.append(halves(mul(y_ts[k], stacked_paths(c_high, c_low))))
            path_high, path_low = path_parts[k]
            left_high = beside(path_high[:64], c_high[:64])
            left_low = beside(path_low[:64], c_low[:64])
            both = beside(i_high[at], env_high[at])
            cross = mul_t(above(left_high, left_low), both)
            cross = cross[:64] + cross[64:]
            cross = cross + mul_t(left_high, beside(i_low[at], env_low[at]))
            total = cross[0:8] * of_center[0]
            for t in range(1, 8):
                total = total + cross[8 * t : 8 * t + 8] * of_center[t]
            grad_angulars.append(total)
        e_high, e_low = split(above(*grad_envs))
        grad_latent = pull + grad_joined[:, :128]
        grad_latent = grad_latent + halves(mul(beside(v_high, e_high), value_t_both))
        grad_latent = grad_latent + mul(beside(v_low, e_low), value_t_high)
        grad_h = grad_latent * u * (gate * (1.0 + h - silu))
        grad_u = pull * update + grad_latent * silu
        h_high, h_low = split(grad_h)
        u_high, u_low = split(grad_u)
        both = mul_t(above(readout_high, readout_low), beside(h_high, u_high))
        grad_scalars.append(
            both[:16] + both[16:] + mul_t(readout_high, beside(h_low, u_low))
        )
    return above(*sums), beside(*grad_scalars), beside(*grad_angulars)


def own_rows(ref, blocks):
    return above(
        *[
            jnp.broadcast_to(ref[pl.ds(block * 8 + t, 1), :], (32, CHANNELS))
            for block in blocks
            for t in range(8)
        ]
    )


def path_rows(path_weight, scale):
    row = iota((72, CHANNELS), 0)
    first, second, third = (path_weight[i : i + 1] for i in range(3))
    return jnp.where(row >= 64, first, jnp.where(row % 8 < 3, second, third)) * scale


def of_kind(species, table):
    result = jnp.zeros(species.shape, F32)
    for kind in range(5):
        result = jnp.where(species == kind, table[0:1, kind : kind + 1], result)
    return result


def column_of(cells):
    rows = above(*[jnp.broadcast_to(cells[i : i + 1], (8, 8)) for i in range(4)])
    own = iota((32, 8), 0) % 8 == iota((32, 8), 1)
    return jnp.sum(jnp.where(own, rows, 0), axis=1, keepdims=True)


def kernel(
    shape,
    positions_hbm, features_hbm, near_hbm,
    species_hbm, centers_hbm, neighbours_hbm, scale_hbm, shift_hbm,
    center_hbm, basis_hbm, path_hbm, value_hbm, latent_hbm, out_hbm,
    listed_hbm, cell_shift_hbm, gather_hbm, scatter_hbm, pick_hbm, domain_hbm, sites_hbm,
    result_ref,
    positions_w, own_w, near_w,
    species_w, centers_w, neighbours_w, scale_w, shift_w,
    center_w, basis_w, path_w, value_w, latent_w, out_w,
    listed_v, cell_shift_v, gather_v, scatter_v, pick_v, domain_v, sites_v,
    mine, message, halo, few, places, returns, outgoing, proj_v, pull_v, ledger,
    local_sem, send_sem, recv_sem,
):
    me = tuple(lax.axis_index(axis) for axis in ("gx", "gy", "gz"))

    def device(direction):
        return tuple(
            lax.rem(i + step + size, size) for i, step, size in zip(me, direction, shape)
        )

    others = [(i, d) for i, d in enumerate(DIRECTIONS) if i != HOME]
    far_first = sorted(others, key=lambda item: -sum(map(abs, item[1])))
    barrier = pltpu.get_barrier_semaphore()
    for _, direction in far_first:
        pl.semaphore_signal(barrier, inc=1, device_id=device(direction), device_id_type=MESH)

    sources = (
        positions_hbm, features_hbm, near_hbm, species_hbm, centers_hbm, neighbours_hbm,
        scale_hbm, shift_hbm, center_hbm, basis_hbm, path_hbm, value_hbm, latent_hbm, out_hbm,
        listed_hbm, cell_shift_hbm, gather_hbm, scatter_hbm, pick_hbm, domain_hbm, sites_hbm,
    )
    targets = (
        positions_w, own_w, near_w, species_w, centers_w, neighbours_w,
        scale_w, shift_w, center_w, basis_w, path_w, value_w, latent_w, out_w,
        listed_v, cell_shift_v, gather_v, scatter_v, pick_v, domain_v, sites_v,
    )
    fetches = [
        pltpu.make_async_copy(src, dst, local_sem.at[i])
        for i, (src, dst) in enumerate(zip(sources, targets))
    ]
    for copy in fetches:
        copy.start()

    slots, starts, order = wanted()
    for copy in fetches[:3]:
        copy.wait()
    own = own_w[...].reshape(32, CHANNELS)
    mine[...] = project(own, near_w[...])
    place = position_row(positions_w[...].reshape(12, 8))
    places[...] = jnp.zeros_like(places)
    places[HOME : HOME + 1, :] = place
    for index, _ in others:
        taken = slots[26 - index]
        done = 0
        while done < len(taken):
            run = 1
            while done + run < len(taken) and taken[done + run] == taken[done] + run:
                run += 1
            message[index, done : done + run] = mine[taken[done] : taken[done] + run]
            done += run
        message[index, done : done + 1] = place
    pl.semaphore_wait(barrier, 26)

    for index, direction in far_first:
        rows = pl.ds(0, len(slots[26 - index]) + 1)
        pltpu.make_async_remote_copy(
            src_ref=message.at[index, rows],
            dst_ref=halo.at[26 - index, rows],
            send_sem=send_sem.at[0],
            recv_sem=recv_sem.at[0],
            device_id=device(direction),
            device_id_type=MESH,
        ).start()

    def settle(rows, semaphore):
        ref = ledger.at[pl.ds(0, rows)]
        pltpu.make_async_copy(ref, ref, semaphore).wait()

    sent_rows = sum(len(slots[i]) + 1 for i, _ in others)

    for copy in fetches[3:]:
        copy.wait()
    live, occupied = listed_pairs(centers_w[...], neighbours_w[...], listed_v[...])
    species = column_of(species_w[...].reshape(4, 8))
    scale = of_kind(species, scale_w[...])
    shift = of_kind(species, shift_w[...])
    pull_v[...] = occupied * scale * out_w[...] * (ROOT_HALF / math.sqrt(32.0))
    proj_v[...] = project(own, center_w[...])
    own_place = sum(mul(part, pick_v[128:256]) for part in split3(by_component(place)))
    base = cell_shift_v[0:3] - own_place[0:3]
    value, latent = value_w[...], latent_w[...]
    weights = (
        split(value) + split(latent) + split(jnp.transpose(latent)) + split(jnp.transpose(value))
    )
    paths = path_rows(path_w[...], 1.0 / math.sqrt(32.0))

    settle(sent_rows, recv_sem.at[0])

    for index, _ in others:
        count = len(slots[index])
        places[index : index + 1, :] = halo[index, count : count + 1]
        if count < 16:
            start = starts[index] - 160
            few[start : start + count, :] = halo[index, 0:count]
    near_rows = above(
        mine[...], *[halo[i, 0 : len(slots[i])] for i in order[1:7]], few[...]
    )
    gathered = sum(mul(part, pick_v[0:128]) for part in split3(by_component(places[...])))
    chosen = above(
        *[
            jnp.sum(gathered[32 * i : 32 * i + 32] * domain_v[...], axis=0, keepdims=True)
            for i in range(3)
        ]
    )
    geo = geometry(chosen + base, live)
    sums, grad_scalars, grad_angular = interactions(
        geo, near_rows, proj_v, pull_v, gather_v, basis_w[...], paths, weights, CHUNK
    )
    grad = pair_gradient(geo, grad_scalars[0:8], grad_scalars[8:9], grad_angular)
    owed = parcels(geo["d"], grad, sites_v[...], scatter_v[...])
    for index in range(27):
        outgoing[index, 0:4] = owed[4 * index : 4 * index + 4]

    rows = pl.ds(0, 4)
    for index, direction in far_first:
        pltpu.make_async_remote_copy(
            src_ref=outgoing.at[index, rows],
            dst_ref=returns.at[26 - index, rows],
            send_sem=send_sem.at[1],
            recv_sem=recv_sem.at[1],
            device_id=device(direction),
            device_id_type=MESH,
        ).start()

    energy = jnp.sum(sums * out_w[...], axis=1, keepdims=True) * (ROOT_HALF / math.sqrt(32.0))
    energy = occupied * (scale * energy + shift)
    at_lane = iota((32, 128), 1) == 96 + iota((32, 128), 0) % 8
    energies = jnp.sum(jnp.where(at_lane, energy, 0.0).reshape(4, 8, 128), axis=1)
    total = outgoing[HOME, 0:4] + energies
    settle(sent_rows, send_sem.at[0])
    settle(104, recv_sem.at[1])
    for index, _ in others:
        total = total + returns[index, 0:4]
    result_ref[0:4, :] = total
    result_ref[4:8, :] = jnp.zeros((4, 128), F32)
    settle(104, send_sem.at[1])


def finish(total_ref, energy_ref, forces_ref, virial_ref):
    total = total_ref[0:4, :]
    energy = total[:, 96:104]
    for cx in range(2):
        energy_ref[cx, 0] = energy[2 * cx : 2 * cx + 2]
    for component in range(3):
        piece = total[:, component * 8 : component * 8 + 8]
        for cx in range(2):
            forces_ref[component, cx, 0] = piece[2 * cx : 2 * cx + 2]
    rows = above(*[jnp.broadcast_to(total[i : i + 1], (8, 128)) for i in range(4)])
    rows = jnp.where(iota((32, 128), 1) % 8 == iota((32, 128), 0) % 8, rows, 0.0)
    fold = (iota((128, 128), 0) // 8 - 3 == iota((128, 128), 1)).astype(F32).astype(BF16)
    by_site = sum(mul(part, fold) for part in split3(rows))
    for cell in range(4):
        virial_ref[cell // 2, 0, cell % 2] = by_site[8 * cell : 8 * cell + 8, 0:9]


def local(shape, *arguments):
    (positions, features, species, centers, neighbours, _, species_scale, species_shift,
     center_weight, near_weight, basis_weight, path_weight, value_weight, latent_weight,
     out_weight) = arguments
    fixed = {name: jnp.asarray(value) for name, value in tables().items()}
    vmem = pl.BlockSpec(memory_space=pltpu.VMEM)
    operands = (
        positions, features, near_weight,
        species, centers.reshape(1, 32), neighbours, species_scale.reshape(1, 5),
        species_shift.reshape(1, 5), center_weight, basis_weight, path_weight, value_weight,
        latent_weight, out_weight.reshape(1, 128),
        fixed["listed"], fixed["shift"], fixed["gather"], fixed["scatter"], fixed["pick"],
        fixed["from_domain"], fixed["sites"],
    )
    total = pl.pallas_call(
        functools.partial(kernel, shape),
        out_shape=jax.ShapeDtypeStruct((8, 128), F32),
        in_specs=[pl.BlockSpec(memory_space=pl.ANY)] * len(operands),
        out_specs=vmem,
        scratch_shapes=[pltpu.VMEM(x.shape, x.dtype) for x in operands]
        + [
            pltpu.VMEM((32, CHANNELS), F32),
            pltpu.VMEM((27, 40, CHANNELS), F32),
            pltpu.VMEM((27, 40, CHANNELS), F32),
            pltpu.VMEM((48, CHANNELS), F32),
            pltpu.VMEM((32, 128), F32),
            pltpu.VMEM((27, 8, 128), F32),
            pltpu.VMEM((27, 8, 128), F32),
            pltpu.VMEM((32, CHANNELS), F32),
            pltpu.VMEM((32, CHANNELS), F32),
            pltpu.VMEM((208, 128), F32),
            pltpu.SemaphoreType.DMA((len(operands),)),
            pltpu.SemaphoreType.DMA((2,)),
            pltpu.SemaphoreType.DMA((2,)),
        ],
        compiler_params=pltpu.CompilerParams(
            collective_id=0, has_side_effects=True, vmem_limit_bytes=56 * 1024 * 1024
        ),
        name="allegro",
    )(*operands)
    energy, forces, virial = pl.pallas_call(
        finish,
        out_shape=(
            jax.ShapeDtypeStruct((2, 1, 2, 8), F32),
            jax.ShapeDtypeStruct((3, 2, 1, 2, 8), F32),
            jax.ShapeDtypeStruct((2, 1, 2, 8, 9), F32),
        ),
        in_specs=[vmem],
        out_specs=(vmem,) * 3,
        name="finish",
    )(total)
    return energy, forces, jnp.transpose(virial, (4, 0, 1, 2, 3))


def solution(mesh):
    placed = (
        P(None, "gx", "gy", "gz", None),
        P("gx", "gy", "gz", None, None),
        P("gx", "gy", "gz", None),
        P(("gx", "gy", "gz")),
        P(("gx", "gy", "gz"), None),
        P(("gx", "gy", "gz")),
    ) + (P(),) * 9
    shape = tuple(mesh.shape[axis] for axis in ("gx", "gy", "gz"))
    return jax.shard_map(
        functools.partial(local, shape),
        mesh=mesh,
        in_specs=placed,
        out_specs=(
            P("gx", "gy", "gz", None),
            P(None, "gx", "gy", "gz", None),
            P(None, "gx", "gy", "gz", None),
        ),
        check_vma=False,
    )
```

time: 41.2 us -> 30.1 us (0.73)
  the two profiles are of different devices: /device:TPU:64 before, /device:TPU:32 now
where the time goes in v2:
time: 30.1 us; the launch traced here: 29.9 us
  Pallas kernels  29.3 us (97%)
  between operations  0.64 us (2%)
    pallas_call x1, Pallas kernels, local(): pl.pallas_call(functools.partial(kernel, shape), out_shape=jax.ShapeDtype...  27.9 us
    pallas_call x1, Pallas kernels, local(): pl.pallas_call(finish, out_shape=(jax.ShapeDtypeStruct((2, 1, 2, 8), F32)...  1.43 us

profile of v2, /device:TPU:32, one launch (start us, length us, event | category | flops | bytes accessed | tf_op | source)
XLA Modules:
  0.0 29.9 jit_solution(14207743555331766254)
XLA Ops:
  0.6 27.9 %allegro.1.total_ref = f32[8,128]{1,0:T(8,128)} custom-call(f32[3,2,1,2,8]{4,3,2,1,0:T(2,128)} %positions_hbm.1, f32[2,1,2,8,128]{4,3,2,1,0:T(8,128)} %features_hbm.1, f32[128,128]{1,0:T(8,128)} %near_hbm.1, s32[2,1,2,8]{3,2,1,0:T(2,128)} %species_hbm.1, s32[1,32]{1,0:T(1,128)} %bitcast.5, s32[32,32]{1,0:T(8,128)} %neighbours_hbm.1, f32[1,5]{1,0:T(1,128)} %bitcast.6, ...), custom_call_target="tpu_custom_call" | custom-call | tf_op jit(solution)/shard_map/allegro/pallas_call | solution.py:596
  28.5 1.4 %finish.1 = (f32[2,1,2,8]{3,2,1,0:T(2,128)}, f32[3,2,1,2,8]{4,3,2,1,0:T(2,128)}, f32[2,1,2,8,9]{4,3,2,1,0:T(8,128)}) custom-call(f32[8,128]{1,0:T(8,128)} %allegro.1.total_ref), custom_call_target="tpu_custom_call" | custom-call | tf_op jit(solution)/shard_map/finish/pallas_call | solution.py:622
